TPU v7x, 32 devices: a whole 2x2x4 slice. The times are simulated.
32 devices in a mesh: mem: 4 (over x, core), slab: 8 (over z, y).
Axes of the slice: x: 2, y: 2, z: 4, core: 2. Of those that a mesh axis runs over, the one named last changes fastest.
Arguments:
- anomalies: bfloat16 [8, 4096, 4096], P('mem', 'slab'), may hold values from -2.390625 to 2.390625
- increment: float32 [4096, 4096], P('slab'), may hold values from -6 to 6
- spectrum: float32 [4096, 4096], P(None, 'slab'), may hold values from 0.01 to 2, as said below
Outputs:
- product: float32 [4096, 4096], P('slab')
Inputs may be any that keep to these rules, and one draw needn't show every extreme that they name: spectrum[k, l] equals spectrum[(4096 - k) % 4096, (4096 - l) % 4096], and is positive.
All inputs are finite; a program needn't handle non-finite values.
Results may differ from a plain program's by a relative error of at most 0.0003.
Values sent between devices are 32-bit elements; how exact they have to be, the bound alone decides.
A program may use at most 192 MiB of HBM per device.

v0:
```python
import math
import jax
import jax.numpy as jnp
from jax import lax
from jax.sharding import PartitionSpec as P


def dft_tables(length, sign):
    first = 1 << (length.bit_length() - 1) // 2
    second = length // first
    index_a = jnp.arange(first, dtype=jnp.int32)
    index_b = jnp.arange(second, dtype=jnp.int32)
    angle_first = (
        2.0 * math.pi / first * (index_a[:, None] * index_a[None, :] % first).astype(jnp.float32)
    )
    angle_twist = (
        2.0 * math.pi / length * (index_a[:, None] * index_b[None, :] % length).astype(jnp.float32)
    )
    angle_second = (
        2.0 * math.pi / second * (index_b[:, None] * index_b[None, :] % second).astype(jnp.float32)
    )
    return (
        first,
        jnp.cos(angle_first),
        sign * jnp.sin(angle_first),
        jnp.cos(angle_twist),
        sign * jnp.sin(angle_twist),
        jnp.cos(angle_second),
        sign * jnp.sin(angle_second),
    )


def complex_section(form, real_part, imag_part, mat_cos, mat_sin):
    highest = lax.Precision.HIGHEST
    out_real = jnp.einsum(form, real_part, mat_cos, precision=highest)
    out_real = out_real - jnp.einsum(form, imag_part, mat_sin, precision=highest)
    out_imag = jnp.einsum(form, real_part, mat_sin, precision=highest)
    out_imag = out_imag + jnp.einsum(form, imag_part, mat_cos, precision=highest)
    return (out_real, out_imag)


def transform(real_part, imag_part, factors, along_last):
    first, first_cos, first_sin, twist_cos, twist_sin, second_cos, second_sin = factors
    shape = real_part.shape
    if along_last:
        blocked = (shape[0], shape[1], first, shape[2] // first)
        form_one, form_two = ("mrab,ac->mrcb", "mrcb,bd->mrdc")
        tw_cos, tw_sin = (twist_cos, twist_sin)
    else:
        blocked = (shape[0], first, shape[1] // first, shape[2])
        form_one, form_two = ("mabk,ac->mcbk", "mcbk,bd->mdck")
        tw_cos, tw_sin = (twist_cos[:, :, None], twist_sin[:, :, None])
    real_part = real_part.reshape(blocked)
    imag_part = imag_part.reshape(blocked)
    step_real, step_imag = complex_section(form_one, real_part, imag_part, first_cos, first_sin)
    twist_real = step_real * tw_cos - step_imag * tw_sin
    twist_imag = step_real * tw_sin + step_imag * tw_cos
    out_real, out_imag = complex_section(form_two, twist_real, twist_imag, second_cos, second_sin)
    out_real = out_real.reshape(shape)
    out_imag = out_imag.reshape(shape)
    return (out_real, out_imag)


def per_device(anomalies, increment, spectrum):
    col_count = anomalies.shape[2]
    row_total = spectrum.shape[0]
    forward_y = dft_tables(col_count, -1.0)
    inverse_y = dft_tables(col_count, 1.0)
    forward_x = dft_tables(row_total, -1.0)
    inverse_x = dft_tables(row_total, 1.0)
    scaled = spectrum * (1.0 / (row_total * col_count))
    fields = anomalies * increment[None]
    wave_real, wave_imag = transform(fields[0::2], fields[1::2], forward_y, True)
    part_real, part_imag = transform(
        lax.all_to_all(wave_real, "slab", split_axis=2, concat_axis=1, tiled=True),
        lax.all_to_all(wave_imag, "slab", split_axis=2, concat_axis=1, tiled=True),
        forward_x,
        False,
    )
    part_real = part_real * scaled[None]
    part_imag = part_imag * scaled[None]
    part_real, part_imag = transform(part_real, part_imag, inverse_x, False)
    back_real = lax.all_to_all(part_real, "slab", split_axis=1, concat_axis=2, tiled=True)
    back_imag = lax.all_to_all(part_imag, "slab", split_axis=1, concat_axis=2, tiled=True)
    even_part, odd_part = transform(back_real, back_imag, inverse_y, True)
    total = jnp.sum(anomalies[0::2] * even_part + anomalies[1::2] * odd_part, axis=0)
    return lax.psum(total, "mem")


def solution(mesh):
    placed = (P("mem", "slab", None), P("slab", None), P(None, "slab"))
    return jax.shard_map(
        per_device, mesh=mesh, in_specs=placed, out_specs=P("slab", None), check_vma=False
    )
```

profile of v0, /device:TPU:0, one launch (start us, length us, event | category | flops | bytes accessed | tf_op | source)
XLA Modules:
  0.0 1516.1 jit_solution(14172679125190159585)
XLA Ops:
  6.7 12.0 copy.122
  27.7 12.1 convert_multiply_fusion
  46.7 13.2 fusion.65
  59.9 13.3 fusion.67
  73.2 13.3 fusion.69
  86.5 24.8 %fusion.6 = (f32[512,64,64]{0,1,2:T(8,128)}, f32[512,64,64]{0,1,2:T(8,128)}) fusion(f32[64,64]{0,1:T(8,128)S(1)} %get-tuple-element.17, f32[64,64]{0,1:T(8,128)S(1)} %get-tuple-element.18, f32[64,512,64]{1,0,2:T(8,128)} %fusion.69, f32[64,512,64]{1,0,2:T(8,128)} %fusion.65, f32[64,512,64]{1,0,2:T(8,128)} %fusion.67, f32[512,64,64]{0,2,1:T(8,128)} %bitcast.203), kind=kOutput, calls=%fused_computation.17 | convolution fusion | flops 1627447296 | bytes 50364416 | tf_op jit(solution)/shard_map/mrab,ac->mrcb/dot_general | solution.py:35
  111.3 16.5 %fusion.57 = f32[64,512,64]{1,0,2:T(8,128)S(1)} fusion(f32[512,64,64]{0,1,2:T(8,128)} %get-tuple-element.12), kind=kOutput, calls=%fused_computation.78 | convolution fusion | flops 1610670080 | bytes 16777216 | tf_op jit(solution)/shard_map/mrcb,bd->mrdc/dot_general | solution.py:38
  127.8 12.0 add_bitcast_fusion.1
  144.8 22.8 %copy.138 = f32[1,512,4096]{1,0,2:T(1,128)} copy(f32[1,512,4096]{1,2,0:T(8,128)S(1)} %bitcast.204) | data formatting | bytes 16777216 | tf_op jit(solution)/shard_map/reshape | solution.py:60
  175.2 16.3 %fusion.59 = f32[64,512,64]{1,0,2:T(8,128)S(1)} fusion(f32[512,64,64]{0,1,2:T(8,128)} %get-tuple-element.12), kind=kOutput, calls=%fused_computation.80 | convolution fusion | flops 1610674176 | bytes 16777216 | tf_op jit(solution)/shard_map/mrcb,bd->mrdc/dot_general | solution.py:36
  191.6 17.2 %subtract_bitcast_fusion.1 = f32[1,512,64,64]{1,2,3,0:T(8,128)S(1)} fusion(f32[64,512,64]{1,0,2:T(8,128)S(1)} %fusion.59, f32[512,64,64]{0,1,2:T(8,128)} %get-tuple-element.11), kind=kOutput, calls=%fused_computation.29 | convolution fusion | flops 1612767232 | bytes 25165824 | tf_op jit(solution)/shard_map/mrcb,bd->mrdc/dot_general | solution.py:35
  213.7 22.8 %copy.132 = f32[1,512,4096]{1,0,2:T(1,128)} copy(f32[1,512,4096]{1,2,0:T(8,128)S(1)} %bitcast.205) | data formatting | bytes 16777216 | tf_op jit(solution)/shard_map/reshape | solution.py:59
  236.5 121.8 %all-to-all-done.1 = f32[1,512,4096]{1,0,2:T(1,128)} async-done(((f32[1,512,4096]{1,0,2:T(1,128)}), f32[1,512,4096]{1,0,2:T(1,128)}, u32[]{:S(2)}, u32[]{:S(2)}) %all-to-all-start.1) | async-done | bytes 8388640 | tf_op jit(solution)/shard_map/all_to_all | solution.py:76
  380.4 17.8 %fusion.49 = f32[64,64,512]{2,0,1:T(8,128)} fusion(f32[64,64,512]{2,1,0:T(8,128)} %bitcast.190), kind=kOutput, calls=%fused_computation.70 | convolution fusion | flops 1610670080 | bytes 16777216 | tf_op jit(solution)/shard_map/mabk,ac->mcbk/dot_general | solution.py:38
  398.2 13.5 fusion.51
  411.7 134.0 %all-to-all-done = f32[1,512,4096]{1,0,2:T(1,128)} async-done(((f32[1,512,4096]{1,0,2:T(1,128)}), f32[1,512,4096]{1,0,2:T(1,128)}, u32[]{:S(2)}, u32[]{:S(2)}) %all-to-all-start) | async-done | bytes 8388640 | tf_op jit(solution)/shard_map/all_to_all | solution.py:75
  562.5 18.1 %fusion.55 = f32[64,64,512]{2,0,1:T(8,128)} fusion(f32[64,64,512]{2,1,0:T(8,128)} %bitcast.196), kind=kOutput, calls=%fused_computation.76 | convolution fusion | flops 1610670080 | bytes 16777216 | tf_op jit(solution)/shard_map/mabk,ac->mcbk/dot_general | solution.py:35
  580.6 24.6 %multiply_subtract_fusion.1 = (f32[64,64,512]{2,0,1:T(8,128)}, f32[64,64,512]{2,0,1:T(8,128)}) fusion(f32[64,64]{0,1:T(8,128)S(1)} %get-tuple-element.17, f32[64,64]{0,1:T(8,128)S(1)} %get-tuple-element.18, f32[64,64,512]{2,0,1:T(8,128)} %fusion.49, f32[64,64,512]{2,0,1:T(8,128)} %fusion.55, f32[64,64,512]{2,0,1:T(8,128)} %fusion.51, ...), kind=kOutput, calls=%fused_computation.27 | convolution fusion | flops 1627451392 | bytes 50364416 | tf_op jit(solution)/shard_map/mabk,ac->mcbk/dot_general | solution.py:37
  605.2 18.4 %fusion.43 = f32[64,64,512]{2,0,1:T(8,128)} fusion(f32[64,64,512]{2,0,1:T(8,128)} %get-tuple-element.10), kind=kOutput, calls=%fused_computation.64 | convolution fusion | flops 1610674176 | bytes 16777216 | tf_op jit(solution)/shard_map/mcbk,bd->mdck/dot_general | solution.py:36
  623.6 12.5 fusion.41
  636.1 15.6 %fusion.77 = f32[64,64,512]{2,0,1:T(8,128)} fusion(f32[64,64,512]{2,0,1:T(8,128)} %fusion.43, f32[64,64,512]{2,0,1:T(8,128)S(1)} %bitcast.183), kind=kOutput, calls=%fused_computation.94 | convolution fusion | flops 1612767232 | bytes 25165824 | tf_op jit(solution)/shard_map/mcbk,bd->mdck/dot_general | solution.py:35
  651.8 11.5 copy.145
  663.3 13.8 fusion.80
  677.1 11.5 copy.149
  688.6 13.8 bitcast_multiply_fusion.6
  702.3 13.2 fusion.33
  715.6 13.3 fusion.35
  728.8 13.2 fusion.39
  742.1 24.8 %multiply_subtract_fusion = (f32[64,64,512]{2,0,1:T(8,128)}, f32[64,64,512]{2,0,1:T(8,128)}) fusion(f32[64,64]{0,1:T(8,128)S(1)} %fusion.152, f32[64,64]{0,1:T(8,128)S(1)} %get-tuple-element.18, f32[64,64,512]{2,0,1:T(8,128)} %fusion.33, f32[64,64,512]{2,0,1:T(8,128)} %fusion.39, f32[64,64,512]{2,0,1:T(8,128)} %fusion.35, f32[64,64,512]{2,1,0:T(8,128)} %bitcast.186), kind=kOutput, calls=%fused_computation.25 | convolution fusion | flops 1627447296 | bytes 50364416 | tf_op jit(solution)/shard_map/mabk,ac->mcbk/dot_general | solution.py:37
  766.9 16.5 %fusion.25 = f32[64,64,512]{2,0,1:T(8,128)S(1)} fusion(f32[64,64,512]{2,0,1:T(8,128)} %get-tuple-element.8), kind=kOutput, calls=%fused_computation.46 | convolution fusion | flops 1610670080 | bytes 16777216 | tf_op jit(solution)/shard_map/mcbk,bd->mdck/dot_general | solution.py:38
  783.4 12.0 fusion.86
  800.5 22.8 %copy.162 = f32[1,4096,512]{2,0,1:T(1,128)} copy(f32[1,4096,512]{2,1,0:T(8,128)S(1)} %bitcast.208) | data formatting | bytes 16777216 | tf_op jit(solution)/shard_map/reshape | solution.py:60
  828.5 16.3 %fusion.27 = f32[64,64,512]{2,0,1:T(8,128)S(1)} fusion(f32[64,64,512]{2,0,1:T(8,128)} %get-tuple-element.8), kind=kOutput, calls=%fused_computation.48 | convolution fusion | flops 1610670080 | bytes 16777216 | tf_op jit(solution)/shard_map/mcbk,bd->mdck/dot_general | solution.py:36
  844.8 17.2 %fusion.83 = f32[64,64,512]{2,0,1:T(8,128)S(1)} fusion(f32[64,64,512]{2,0,1:T(8,128)S(1)} %fusion.27, f32[64,64,512]{2,0,1:T(8,128)} %get-tuple-element.7), kind=kOutput, calls=%fused_computation.96 | convolution fusion | flops 1612767232 | bytes 25165824 | tf_op jit(solution)/shard_map/mcbk,bd->mdck/dot_general | solution.py:35
  866.9 22.8 %copy.156 = f32[1,4096,512]{2,0,1:T(1,128)} copy(f32[1,4096,512]{2,1,0:T(8,128)S(1)} %bitcast.209) | data formatting | bytes 16777216 | tf_op jit(solution)/shard_map/reshape | solution.py:59
  889.7 120.7 %all-to-all-done.3 = f32[1,4096,512]{2,0,1:T(1,128)} async-done(((f32[1,4096,512]{2,0,1:T(1,128)}), f32[1,4096,512]{2,0,1:T(1,128)}, u32[]{:S(2)}, u32[]{:S(2)}) %all-to-all-start.3) | async-done | bytes 8388640 | tf_op jit(solution)/shard_map/all_to_all | solution.py:84
  1032.4 17.8 %fusion.17 = f32[64,512,64]{1,0,2:T(8,128)} fusion(f32[512,64,64]{0,2,1:T(8,128)} %bitcast.192), kind=kOutput, calls=%fused_computation.38 | convolution fusion | flops 1610670080 | bytes 16777216 | tf_op jit(solution)/shard_map/mrab,ac->mrcb/dot_general | solution.py:38
  1050.2 13.4 fusion.19
  1063.5 134.1 %all-to-all-done.2 = f32[1,4096,512]{2,0,1:T(1,128)} async-done(((f32[1,4096,512]{2,0,1:T(1,128)}), f32[1,4096,512]{2,0,1:T(1,128)}, u32[]{:S(2)}, u32[]{:S(2)}) %all-to-all-start.2) | async-done | bytes 8388640 | tf_op jit(solution)/shard_map/all_to_all | solution.py:83
  1214.4 18.1 %fusion.21 = f32[64,512,64]{1,0,2:T(8,128)} fusion(f32[512,64,64]{0,2,1:T(8,128)} %bitcast.194), kind=kOutput, calls=%fused_computation.42 | convolution fusion | flops 1610670080 | bytes 16777216 | tf_op jit(solution)/shard_map/mrab,ac->mrcb/dot_general | solution.py:37
  1232.4 24.5 %fusion.2 = (f32[512,64,64]{0,1,2:T(8,128)}, f32[512,64,64]{0,1,2:T(8,128)}) fusion(f32[64,64]{0,1:T(8,128)S(1)} %fusion.152, f32[64,64]{0,1:T(8,128)S(1)} %get-tuple-element.18, f32[64,512,64]{1,0,2:T(8,128)} %fusion.21, f32[64,512,64]{1,0,2:T(8,128)} %fusion.17, f32[64,512,64]{1,0,2:T(8,128)} %fusion.19, f32[512,64,64]{0,2,1:T(8,128)} %bitcast.195), kind=kOutput, calls=%fused_computation.7 | convolution fusion | flops 1627447296 | bytes 50364416 | tf_op jit(solution)/shard_map/mrab,ac->mrcb/dot_general | solution.py:35
  1257.0 17.0 %fusion.11 = f32[64,512,64]{1,0,2:T(8,128)S(1)} fusion(f32[512,64,64]{0,1,2:T(8,128)} %get-tuple-element.6), kind=kOutput, calls=%fused_computation.32 | convolution fusion | flops 1610670080 | bytes 16777216 | tf_op jit(solution)/shard_map/mrcb,bd->mrdc/dot_general | solution.py:36
  1274.0 13.5 fusion.9
  1287.5 13.7 subtract_bitcast_fusion
  1301.3 11.7 copy.169
  1313.0 15.6 %add_bitcast_fusion = f32[1,512,64,64]{1,2,3,0:T(8,128)} fusion(f32[64,512,64]{1,0,2:T(8,128)} %fusion.9, f32[512,64,64]{0,1,2:T(8,128)S(1)} %bitcast.181), kind=kOutput, calls=%fused_computation.22 | convolution fusion | flops 1612767232 | bytes 25165824 | tf_op jit(solution)/shard_map/mrcb,bd->mrdc/dot_general | solution.py:37
  1328.6 11.7 copy.173
  1347.9 152.2 %all-reduce.2.cloned.1.call-done = f32[512,4096]{0,1:T(8,128)} async-done(((f32[512,4096]{0,1:T(8,128)}), f32[512,4096]{0,1:T(8,128)}) %all-reduce.2.cloned.1.call-update) | async-done | bytes 8388624 | tf_op jit(solution)/shard_map/psum | solution.py:87
  (60 shorter events, 142.8 us)
Async XLA Ops:
  46.7 26.6 %copy-start.6 = (f32[1,512,4096]{1,2,0:T(8,128)}, f32[1,512,4096]{1,2,0:T(8,128)S(1)}, u32[]{:S(2)}) copy-start(f32[1,512,4096]{1,2,0:T(8,128)S(1)} %get-tuple-element.14) | copy-start | bytes 25165828
  111.3 16.5 %copy-start = (f32[512,64,64]{0,1,2:T(8,128)S(1)}, f32[512,64,64]{0,1,2:T(8,128)}, u32[]{:S(2)}) copy-start(f32[512,64,64]{0,1,2:T(8,128)} %get-tuple-element.11) | copy-start | bytes 25165828
  167.6 190.7 %all-to-all-start.1 = ((f32[1,512,4096]{1,0,2:T(1,128)}), f32[1,512,4096]{1,0,2:T(1,128)}, u32[]{:S(2)}, u32[]{:S(2)}) async-start(f32[1,512,4096]{1,0,2:T(1,128)} %copy.138), calls=%async_computation.1 | async-start | bytes 16777216 | tf_op jit(solution)/shard_map/all_to_all | solution.py:76
  358.3 187.4 %all-to-all-start = ((f32[1,512,4096]{1,0,2:T(1,128)}), f32[1,512,4096]{1,0,2:T(1,128)}, u32[]{:S(2)}, u32[]{:S(2)}) async-start(f32[1,512,4096]{1,0,2:T(1,128)} %copy.132), calls=%async_computation | async-start | bytes 16777216 | tf_op jit(solution)/shard_map/all_to_all | solution.py:75
  380.4 17.8 %copy-start.2 = (f32[1,8,512,512]{3,2,1,0:T(8,128)S(1)}, f32[1,8,512,512]{3,2,1,0:T(8,128)}, u32[]{:S(2)}) copy-start(f32[1,8,512,512]{3,2,1,0:T(8,128)} %copy.139) | copy-start | bytes 25165828
  605.2 18.4 %copy-start.5 = (f32[64,64,512]{2,0,1:T(8,128)S(1)}, f32[64,64,512]{2,0,1:T(8,128)}, u32[]{:S(2)}) copy-start(f32[64,64,512]{2,0,1:T(8,128)} %get-tuple-element.10) | copy-start | bytes 25165828
  605.2 30.9 %slice-start.2 = ((s8[8388608]{0:T(1024)(128)(4,1)}), s8[4194304]{0:T(1024)(128)(4,1)S(1)}, s32[]{:S(2)}) async-start(s8[8388608]{0:T(1024)(128)(4,1)} %bitcast.182), calls=%async_computation.7 | async-start | bytes 8388608
  623.6 12.5 slice-start.3
  702.3 26.5 %slice-start.4 = ((s8[8388608]{0:T(1024)(128)(4,1)}), s8[4194304]{0:T(1024)(128)(4,1)S(1)}, s32[]{:S(2)}) async-start(s8[8388608]{0:T(1024)(128)(4,1)} %bitcast.187), calls=%async_computation.9 | async-start | bytes 8388608
  715.6 13.3 slice-start.5
  766.9 16.5 %copy-start.1 = (f32[64,64,512]{2,0,1:T(8,128)S(1)}, f32[64,64,512]{2,0,1:T(8,128)}, u32[]{:S(2)}) copy-start(f32[64,64,512]{2,0,1:T(8,128)} %get-tuple-element.7) | copy-start | bytes 25165828
  823.3 187.2 %all-to-all-start.3 = ((f32[1,4096,512]{2,0,1:T(1,128)}), f32[1,4096,512]{2,0,1:T(1,128)}, u32[]{:S(2)}, u32[]{:S(2)}) async-start(f32[1,4096,512]{2,0,1:T(1,128)} %copy.162), calls=%async_computation.3 | async-start | bytes 16777216 | tf_op jit(solution)/shard_map/all_to_all | solution.py:84
  1010.4 187.2 %all-to-all-start.2 = ((f32[1,4096,512]{2,0,1:T(1,128)}), f32[1,4096,512]{2,0,1:T(1,128)}, u32[]{:S(2)}, u32[]{:S(2)}) async-start(f32[1,4096,512]{2,0,1:T(1,128)} %copy.156), calls=%async_computation.2 | async-start | bytes 16777216 | tf_op jit(solution)/shard_map/all_to_all | solution.py:83
  1015.4 484.7 %all-reduce.2.cloned.1.call-start = ((), (), s32[]{:S(2)}) async-start(), calls=%async_computation.4 | async-start | bytes 16777216 | tf_op jit(solution)/shard_map/psum | solution.py:87
  1032.4 17.8 %copy-start.3 = (f32[1,512,8,512]{1,3,2,0:T(8,128)S(1)}, f32[1,512,8,512]{1,3,2,0:T(8,128)}, u32[]{:S(2)}) copy-start(f32[1,512,8,512]{1,3,2,0:T(8,128)} %copy.163) | copy-start | bytes 25165828
  1256.9 17.0 %copy-start.4 = (f32[512,64,64]{0,1,2:T(8,128)S(1)}, f32[512,64,64]{0,1,2:T(8,128)}, u32[]{:S(2)}) copy-start(f32[512,64,64]{0,1,2:T(8,128)} %get-tuple-element.6) | copy-start | bytes 25165828
  1256.9 30.6 %slice-start = ((s8[8388608]{0:T(1024)(128)(4,1)}), s8[4194304]{0:T(1024)(128)(4,1)S(1)}, s32[]{:S(2)}) async-start(s8[8388608]{0:T(1024)(128)(4,1)} %bitcast.180), calls=%async_computation.5 | async-start | bytes 8388608
  1274.0 13.5 slice-start.1
  1301.3 39.0 %slice-start.6 = ((s8[8388608]{0:T(1024)(128)(4,1)}), s8[4194304]{0:T(1024)(128)(4,1)S(1)}, s32[]{:S(2)}) async-start(s8[8388608]{0:T(1024)(128)(4,1)} %bitcast.200), calls=%async_computation.11 | async-start | bytes 8388608
  1313.0 27.3 %slice-start.7 = ((s8[8388608]{0:T(1024)(128)(4,1)}), s8[4194304]{0:T(1024)(128)(4,1)S(1)}, s32[]{:S(2)}) async-start(s8[8388608]{0:T(1024)(128)(4,1)} %bitcast.200), calls=%async_computation.12 | async-start | bytes 8388608
  1328.6 11.7 copy-start.7
Sparse Core Ops, SparseCore 0:
  1348.0 152.0 all-reduce.1
where the time goes:
time: 1520 us
  waiting for transfers between devices  663 us (44%)
  matrix products  521 us (34%)
  local copies, waits for them, and re-layouts  261 us (17%)
  other arithmetic  33.7 us (2%)
  starting transfers between devices  23 us (2%)
    psum x1, waiting for transfers between devices, per_device(): return lax.psum(total, 'mem')  152 us
    dot_general x8, matrix products, complex_section(): out_real = jnp.einsum(form, real_part, mat_cos, precision=highest)  144 us
    dot_general x8, matrix products, complex_section(): out_imag = jnp.einsum(form, real_part, mat_sin, precision=highest)  134 us
    all_to_all x1, waiting for transfers between devices, per_device(): lax.all_to_all(part_real, 'slab', split_axis=1, concat_axis=2, tiled=True)  134 us
    all_to_all x1, waiting for transfers between devices, per_device(): lax.all_to_all(wave_real, 'slab', split_axis=2, concat_axis=1, tiled=True)  134 us
    all_to_all x1, waiting for transfers between devices, per_device(): lax.all_to_all(wave_imag, 'slab', split_axis=2, concat_axis=1, tiled=True)  122 us
    dot_general x8, matrix products, complex_section(): jnp.einsum(form, imag_part, mat_sin, precision=highest)  121 us
    dot_general x8, matrix products, complex_section(): jnp.einsum(form, imag_part, mat_cos, precision=highest)  121 us
  transfers between devices with their start and end apart: 5, of which 5 were waited for; matrix products, arithmetic and copies ran while one was open for 14% of the time, Pallas kernels for 0%

commit v1 on v0

--- a/solution.py
+++ b/solution.py
@@ -80,7 +80,9 @@
     part_real = part_real * scaled[None]
     part_imag = part_imag * scaled[None]
     part_real, part_imag = transform(part_real, part_imag, inverse_x, False)
-    back_real = lax.all_to_all(part_real, "slab", split_axis=1, concat_axis=2, tiled=True)
+    pieces = jnp.split(part_real, lax.axis_size("slab"), axis=1)
+    got = lax.all_to_all(jnp.stack(pieces), "slab", 0, 0)
+    back_real = jnp.concatenate(got, axis=2)
     back_imag = lax.all_to_all(part_imag, "slab", split_axis=1, concat_axis=2, tiled=True)
     even_part, odd_part = transform(back_real, back_imag, inverse_y, True)
     total = jnp.sum(anomalies[0::2] * even_part + anomalies[1::2] * odd_part, axis=0)

time: 1520 us -> 1520 us (level)
  local copies, waits for them, and re-layouts: 261 us -> 239 us
    reshape x2 -> x1, local copies, waits for them, and re-layouts: 45.6 us -> 22.8 us  [transform(): out_real = out_real.reshape(shape)]
    unnamed x38 -> x44, local copies, waits for them, and re-layouts: 51.5 us -> 51.2 us
where the time goes in v1:
time: 1520 us; the launch traced here: 1510 us
  waiting for transfers between devices  677 us (45%)
  matrix products  522 us (34%)
  local copies, waits for them, and re-layouts  239 us (16%)
  other arithmetic  33.7 us (2%)
  starting transfers between devices  23 us (2%)
    psum x1, waiting for transfers between devices, per_device(): return lax.psum(total, 'mem')  152 us
    dot_general x8, matrix products, complex_section(): out_real = jnp.einsum(form, real_part, mat_cos, precision=highest)  145 us
    all_to_all x1, waiting for transfers between devices, per_device(): lax.all_to_all(part_imag, 'slab', split_axis=1, concat_axis=2, tiled=True)  135 us
    all_to_all x1, waiting for transfers between devices, per_device(): lax.all_to_all(wave_real, 'slab', split_axis=2, concat_axis=1, tiled=True)  134 us
    dot_general x8, matrix products, complex_section(): out_imag = jnp.einsum(form, real_part, mat_sin, precision=highest)  134 us
    all_to_all x1, waiting for transfers between devices, per_device(): got = lax.all_to_all(jnp.stack(pieces), 'slab', 0, 0)  134 us
    all_to_all x1, waiting for transfers between devices, per_device(): lax.all_to_all(wave_imag, 'slab', split_axis=2, concat_axis=1, tiled=True)  122 us
    dot_general x8, matrix products, complex_section(): jnp.einsum(form, imag_part, mat_sin, precision=highest)  122 us
  transfers between devices with their start and end apart: 5, of which 5 were waited for; matrix products, arithmetic and copies ran while one was open for 14% of the time, Pallas kernels for 0%

profile of v1, /device:TPU:0, one launch (start us, length us, event | category | flops | bytes accessed | tf_op | source)
XLA Modules:
  0.0 1508.9 jit_solution(3775833564742034415)
XLA Ops:
  6.7 12.0 copy.122
  27.7 12.1 convert_multiply_fusion
  46.7 13.3 fusion.65
  59.9 13.3 fusion.67
  73.3 13.3 fusion.69
  86.5 24.8 %fusion.6 = (f32[512,64,64]{0,1,2:T(8,128)}, f32[512,64,64]{0,1,2:T(8,128)}) fusion(f32[64,64]{0,1:T(8,128)S(1)} %get-tuple-element.17, f32[64,64]{0,1:T(8,128)S(1)} %get-tuple-element.18, f32[64,512,64]{1,0,2:T(8,128)} %fusion.69, f32[64,512,64]{1,0,2:T(8,128)} %fusion.65, f32[64,512,64]{1,0,2:T(8,128)} %fusion.67, f32[512,64,64]{0,2,1:T(8,128)} %bitcast.233), kind=kOutput, calls=%fused_computation.17 | convolution fusion | flops 1627447296 | bytes 50364416 | tf_op jit(solution)/shard_map/mrab,ac->mrcb/dot_general | solution.py:35
  111.4 16.5 %fusion.57 = f32[64,512,64]{1,0,2:T(8,128)S(1)} fusion(f32[512,64,64]{0,1,2:T(8,128)} %get-tuple-element.12), kind=kOutput, calls=%fused_computation.78 | convolution fusion | flops 1610670080 | bytes 16777216 | tf_op jit(solution)/shard_map/mrcb,bd->mrdc/dot_general | solution.py:38
  127.9 12.0 add_bitcast_fusion.1
  144.9 22.8 %copy.138 = f32[1,512,4096]{1,0,2:T(1,128)} copy(f32[1,512,4096]{1,2,0:T(8,128)S(1)} %bitcast.242) | data formatting | bytes 16777216 | tf_op jit(solution)/shard_map/reshape | solution.py:60
  175.3 16.3 %fusion.59 = f32[64,512,64]{1,0,2:T(8,128)S(1)} fusion(f32[512,64,64]{0,1,2:T(8,128)} %get-tuple-element.12), kind=kOutput, calls=%fused_computation.80 | convolution fusion | flops 1610674176 | bytes 16777216 | tf_op jit(solution)/shard_map/mrcb,bd->mrdc/dot_general | solution.py:36
  191.7 17.2 %subtract_bitcast_fusion.1 = f32[1,512,64,64]{1,2,3,0:T(8,128)S(1)} fusion(f32[64,512,64]{1,0,2:T(8,128)S(1)} %fusion.59, f32[512,64,64]{0,1,2:T(8,128)} %get-tuple-element.11), kind=kOutput, calls=%fused_computation.29 | convolution fusion | flops 1612767232 | bytes 25165824 | tf_op jit(solution)/shard_map/mrcb,bd->mrdc/dot_general | solution.py:35
  213.8 22.8 %copy.132 = f32[1,512,4096]{1,0,2:T(1,128)} copy(f32[1,512,4096]{1,2,0:T(8,128)S(1)} %bitcast.243) | data formatting | bytes 16777216 | tf_op jit(solution)/shard_map/reshape | solution.py:59
  236.6 121.8 %all-to-all-done.1 = f32[1,512,4096]{1,0,2:T(1,128)} async-done(((f32[1,512,4096]{1,0,2:T(1,128)}), f32[1,512,4096]{1,0,2:T(1,128)}, u32[]{:S(2)}, u32[]{:S(2)}) %all-to-all-start.1) | async-done | bytes 8388640 | tf_op jit(solution)/shard_map/all_to_all | solution.py:76
  380.5 17.8 %fusion.49 = f32[64,64,512]{2,0,1:T(8,128)} fusion(f32[64,64,512]{2,1,0:T(8,128)} %bitcast.220), kind=kOutput, calls=%fused_computation.70 | convolution fusion | flops 1610670080 | bytes 16777216 | tf_op jit(solution)/shard_map/mabk,ac->mcbk/dot_general | solution.py:38
  398.3 13.5 fusion.51
  411.8 134.0 %all-to-all-done = f32[1,512,4096]{1,0,2:T(1,128)} async-done(((f32[1,512,4096]{1,0,2:T(1,128)}), f32[1,512,4096]{1,0,2:T(1,128)}, u32[]{:S(2)}, u32[]{:S(2)}) %all-to-all-start) | async-done | bytes 8388640 | tf_op jit(solution)/shard_map/all_to_all | solution.py:75
  562.6 18.1 %fusion.55 = f32[64,64,512]{2,0,1:T(8,128)} fusion(f32[64,64,512]{2,1,0:T(8,128)} %bitcast.226), kind=kOutput, calls=%fused_computation.76 | convolution fusion | flops 1610670080 | bytes 16777216 | tf_op jit(solution)/shard_map/mabk,ac->mcbk/dot_general | solution.py:35
  580.7 24.6 %multiply_subtract_fusion.1 = (f32[64,64,512]{2,0,1:T(8,128)}, f32[64,64,512]{2,0,1:T(8,128)}) fusion(f32[64,64]{0,1:T(8,128)S(1)} %get-tuple-element.17, f32[64,64]{0,1:T(8,128)S(1)} %get-tuple-element.18, f32[64,64,512]{2,0,1:T(8,128)} %fusion.49, f32[64,64,512]{2,0,1:T(8,128)} %fusion.55, f32[64,64,512]{2,0,1:T(8,128)} %fusion.51, ...), kind=kOutput, calls=%fused_computation.27 | convolution fusion | flops 1627451392 | bytes 50364416 | tf_op jit(solution)/shard_map/mabk,ac->mcbk/dot_general | solution.py:37
  605.3 18.4 %fusion.43 = f32[64,64,512]{2,0,1:T(8,128)} fusion(f32[64,64,512]{2,0,1:T(8,128)} %get-tuple-element.10), kind=kOutput, calls=%fused_computation.64 | convolution fusion | flops 1610674176 | bytes 16777216 | tf_op jit(solution)/shard_map/mcbk,bd->mdck/dot_general | solution.py:36
  623.7 12.5 fusion.41
  636.2 15.6 %fusion.77 = f32[64,64,512]{2,0,1:T(8,128)} fusion(f32[64,64,512]{2,0,1:T(8,128)} %fusion.43, f32[64,64,512]{2,0,1:T(8,128)S(1)} %bitcast.213), kind=kOutput, calls=%fused_computation.94 | convolution fusion | flops 1612767232 | bytes 25165824 | tf_op jit(solution)/shard_map/mcbk,bd->mdck/dot_general | solution.py:35
  651.9 11.5 copy.145
  663.3 13.8 fusion.80
  677.1 11.5 copy.149
  688.7 13.8 bitcast_multiply_fusion.6
  702.4 13.2 fusion.33
  715.6 13.3 fusion.35
  728.9 13.2 fusion.39
  742.2 24.8 %multiply_subtract_fusion = (f32[64,64,512]{2,0,1:T(8,128)}, f32[64,64,512]{2,0,1:T(8,128)}) fusion(f32[64,64]{0,1:T(8,128)S(1)} %fusion.160, f32[64,64]{0,1:T(8,128)S(1)} %get-tuple-element.18, f32[64,64,512]{2,0,1:T(8,128)} %fusion.33, f32[64,64,512]{2,0,1:T(8,128)} %fusion.39, f32[64,64,512]{2,0,1:T(8,128)} %fusion.35, f32[64,64,512]{2,1,0:T(8,128)} %bitcast.216), kind=kOutput, calls=%fused_computation.25 | convolution fusion | flops 1627447296 | bytes 50364416 | tf_op jit(solution)/shard_map/mabk,ac->mcbk/dot_general | solution.py:37
  767.0 16.5 %fusion.25 = f32[64,64,512]{2,0,1:T(8,128)S(1)} fusion(f32[64,64,512]{2,0,1:T(8,128)} %get-tuple-element.8), kind=kOutput, calls=%fused_computation.46 | convolution fusion | flops 1610670080 | bytes 16777216 | tf_op jit(solution)/shard_map/mcbk,bd->mdck/dot_general | solution.py:38
  783.5 12.0 fusion.86
  800.6 22.8 %copy.161 = f32[1,4096,512]{2,0,1:T(1,128)} copy(f32[1,4096,512]{2,1,0:T(8,128)S(1)} %bitcast.246) | data formatting | bytes 16777216 | tf_op jit(solution)/shard_map/reshape | solution.py:60
  828.6 16.3 %fusion.27 = f32[64,64,512]{2,0,1:T(8,128)S(1)} fusion(f32[64,64,512]{2,0,1:T(8,128)} %get-tuple-element.8), kind=kOutput, calls=%fused_computation.48 | convolution fusion | flops 1610670080 | bytes 16777216 | tf_op jit(solution)/shard_map/mcbk,bd->mdck/dot_general | solution.py:36
  844.9 17.7 %fusion.83 = f32[64,64,512]{2,0,1:T(8,128)S(1)} fusion(f32[64,64,512]{2,0,1:T(8,128)S(1)} %fusion.27, f32[64,64,512]{2,0,1:T(8,128)} %get-tuple-element.7), kind=kOutput, calls=%fused_computation.96 | convolution fusion | flops 1612767232 | bytes 25165824 | tf_op jit(solution)/shard_map/mcbk,bd->mdck/dot_general | solution.py:35
  875.9 134.6 %all-to-all-done.3 = f32[1,4096,512]{2,0,1:T(1,128)} async-done(((f32[1,4096,512]{2,0,1:T(1,128)}), f32[1,4096,512]{2,0,1:T(1,128)}, u32[]{:S(2)}, u32[]{:S(2)}) %all-to-all-start.3) | async-done | bytes 8388640 | tf_op jit(solution)/shard_map/all_to_all | solution.py:86
  1023.2 9.3 copy.162
  1032.5 17.8 %fusion.17 = f32[64,512,64]{1,0,2:T(8,128)} fusion(f32[512,64,64]{0,2,1:T(8,128)} %bitcast.222), kind=kOutput, calls=%fused_computation.38 | convolution fusion | flops 1610670080 | bytes 16777216 | tf_op jit(solution)/shard_map/mrab,ac->mrcb/dot_general | solution.py:38
  1050.3 13.5 fusion.19
  1063.8 133.9 %all-to-all-done.2 = f32[8,1,512,512]{3,2,1,0:T(8,128)} async-done(((f32[8,1,512,512]{3,2,1,0:T(8,128)}), f32[8,1,512,512]{3,2,1,0:T(8,128)}, u32[]{:S(2)}, u32[]{:S(2)}) %all-to-all-start.2) | async-done | bytes 8388640 | tf_op jit(solution)/shard_map/all_to_all | solution.py:84
  1206.8 17.8 %fusion.21 = f32[64,512,64]{1,0,2:T(8,128)} fusion(f32[512,64,64]{0,2,1:T(8,128)} %bitcast.224), kind=kOutput, calls=%fused_computation.42 | convolution fusion | flops 1610670080 | bytes 16777216 | tf_op jit(solution)/shard_map/mrab,ac->mrcb/dot_general | solution.py:37
  1224.6 24.9 %fusion.2 = (f32[512,64,64]{0,1,2:T(8,128)}, f32[512,64,64]{0,1,2:T(8,128)}) fusion(f32[64,64]{0,1:T(8,128)S(1)} %fusion.160, f32[64,64]{0,1:T(8,128)S(1)} %get-tuple-element.18, f32[64,512,64]{1,0,2:T(8,128)} %fusion.21, f32[64,512,64]{1,0,2:T(8,128)} %fusion.17, f32[64,512,64]{1,0,2:T(8,128)} %fusion.19, f32[512,64,64]{0,2,1:T(8,128)} %bitcast.225), kind=kOutput, calls=%fused_computation.7 | convolution fusion | flops 1627447296 | bytes 50364416 | tf_op jit(solution)/shard_map/mrab,ac->mrcb/dot_general | solution.py:35
  1249.5 17.0 %fusion.11 = f32[64,512,64]{1,0,2:T(8,128)S(1)} fusion(f32[512,64,64]{0,1,2:T(8,128)} %get-tuple-element.6), kind=kOutput, calls=%fused_computation.32 | convolution fusion | flops 1610670080 | bytes 16777216 | tf_op jit(solution)/shard_map/mrcb,bd->mrdc/dot_general | solution.py:36
  1266.5 13.3 fusion.9
  1279.9 13.8 subtract_bitcast_fusion
  1293.7 11.7 copy.168
  1305.4 15.7 %add_bitcast_fusion = f32[1,512,64,64]{1,2,3,0:T(8,128)} fusion(f32[64,512,64]{1,0,2:T(8,128)} %fusion.9, f32[512,64,64]{0,1,2:T(8,128)S(1)} %bitcast.211), kind=kOutput, calls=%fused_computation.22 | convolution fusion | flops 1612767232 | bytes 25165824 | tf_op jit(solution)/shard_map/mrcb,bd->mrdc/dot_general | solution.py:37
  1321.1 11.7 copy.172
  1340.4 152.3 %all-reduce.2.cloned.1.call-done = f32[512,4096]{0,1:T(8,128)} async-done(((f32[512,4096]{0,1:T(8,128)}), f32[512,4096]{0,1:T(8,128)}) %all-reduce.2.cloned.1.call-update) | async-done | bytes 8388624 | tf_op jit(solution)/shard_map/psum | solution.py:89
  (66 shorter events, 134.2 us)
Async XLA Ops:
  46.7 26.6 %copy-start.6 = (f32[1,512,4096]{1,2,0:T(8,128)}, f32[1,512,4096]{1,2,0:T(8,128)S(1)}, u32[]{:S(2)}) copy-start(f32[1,512,4096]{1,2,0:T(8,128)S(1)} %get-tuple-element.14) | copy-start | bytes 25165828
  111.4 16.5 %copy-start = (f32[512,64,64]{0,1,2:T(8,128)S(1)}, f32[512,64,64]{0,1,2:T(8,128)}, u32[]{:S(2)}) copy-start(f32[512,64,64]{0,1,2:T(8,128)} %get-tuple-element.11) | copy-start | bytes 25165828
  167.7 190.7 %all-to-all-start.1 = ((f32[1,512,4096]{1,0,2:T(1,128)}), f32[1,512,4096]{1,0,2:T(1,128)}, u32[]{:S(2)}, u32[]{:S(2)}) async-start(f32[1,512,4096]{1,0,2:T(1,128)} %copy.138), calls=%async_computation.1 | async-start | bytes 16777216 | tf_op jit(solution)/shard_map/all_to_all | solution.py:76
  358.4 187.4 %all-to-all-start = ((f32[1,512,4096]{1,0,2:T(1,128)}), f32[1,512,4096]{1,0,2:T(1,128)}, u32[]{:S(2)}, u32[]{:S(2)}) async-start(f32[1,512,4096]{1,0,2:T(1,128)} %copy.132), calls=%async_computation | async-start | bytes 16777216 | tf_op jit(solution)/shard_map/all_to_all | solution.py:75
  380.5 17.8 %copy-start.2 = (f32[1,8,512,512]{3,2,1,0:T(8,128)S(1)}, f32[1,8,512,512]{3,2,1,0:T(8,128)}, u32[]{:S(2)}) copy-start(f32[1,8,512,512]{3,2,1,0:T(8,128)} %copy.139) | copy-start | bytes 25165828
  605.3 18.4 %copy-start.5 = (f32[64,64,512]{2,0,1:T(8,128)S(1)}, f32[64,64,512]{2,0,1:T(8,128)}, u32[]{:S(2)}) copy-start(f32[64,64,512]{2,0,1:T(8,128)} %get-tuple-element.10) | copy-start | bytes 25165828
  605.3 30.9 %slice-start.2 = ((s8[8388608]{0:T(1024)(128)(4,1)}), s8[4194304]{0:T(1024)(128)(4,1)S(1)}, s32[]{:S(2)}) async-start(s8[8388608]{0:T(1024)(128)(4,1)} %bitcast.212), calls=%async_computation.7 | async-start | bytes 8388608
  623.7 12.5 slice-start.3
  702.4 26.5 %slice-start.4 = ((s8[8388608]{0:T(1024)(128)(4,1)}), s8[4194304]{0:T(1024)(128)(4,1)S(1)}, s32[]{:S(2)}) async-start(s8[8388608]{0:T(1024)(128)(4,1)} %bitcast.217), calls=%async_computation.9 | async-start | bytes 8388608
  715.6 13.3 slice-start.5
  767.0 16.5 %copy-start.1 = (f32[64,64,512]{2,0,1:T(8,128)S(1)}, f32[64,64,512]{2,0,1:T(8,128)}, u32[]{:S(2)}) copy-start(f32[64,64,512]{2,0,1:T(8,128)} %get-tuple-element.7) | copy-start | bytes 25165828
  823.4 187.1 %all-to-all-start.3 = ((f32[1,4096,512]{2,0,1:T(1,128)}), f32[1,4096,512]{2,0,1:T(1,128)}, u32[]{:S(2)}, u32[]{:S(2)}) async-start(f32[1,4096,512]{2,0,1:T(1,128)} %copy.161), calls=%async_computation.3 | async-start | bytes 16777216 | tf_op jit(solution)/shard_map/all_to_all | solution.py:86
  1010.5 187.2 %all-to-all-start.2 = ((f32[8,1,512,512]{3,2,1,0:T(8,128)}), f32[8,1,512,512]{3,2,1,0:T(8,128)}, u32[]{:S(2)}, u32[]{:S(2)}) async-start(f32[8,1,512,512]{3,2,1,0:T(8,128)} %fusion.93), calls=%async_computation.2 | async-start | bytes 16777216 | tf_op jit(solution)/shard_map/all_to_all | solution.py:84
  1015.5 477.1 %all-reduce.2.cloned.1.call-start = ((), (), s32[]{:S(2)}) async-start(), calls=%async_computation.4 | async-start | bytes 16777216 | tf_op jit(solution)/shard_map/psum | solution.py:89
  1032.5 17.8 %copy-start.3 = (f32[1,512,8,512]{1,3,2,0:T(8,128)S(1)}, f32[1,512,8,512]{1,3,2,0:T(8,128)}, u32[]{:S(2)}) copy-start(f32[1,512,8,512]{1,3,2,0:T(8,128)} %copy.162) | copy-start | bytes 25165828
  1249.5 17.0 %copy-start.4 = (f32[512,64,64]{0,1,2:T(8,128)S(1)}, f32[512,64,64]{0,1,2:T(8,128)}, u32[]{:S(2)}) copy-start(f32[512,64,64]{0,1,2:T(8,128)} %get-tuple-element.6) | copy-start | bytes 25165828
  1249.5 30.4 %slice-start = ((s8[8388608]{0:T(1024)(128)(4,1)}), s8[4194304]{0:T(1024)(128)(4,1)S(1)}, s32[]{:S(2)}) async-start(s8[8388608]{0:T(1024)(128)(4,1)} %bitcast.210), calls=%async_computation.5 | async-start | bytes 8388608
  1266.5 13.4 slice-start.1
  1293.7 39.1 %slice-start.6 = ((s8[8388608]{0:T(1024)(128)(4,1)}), s8[4194304]{0:T(1024)(128)(4,1)S(1)}, s32[]{:S(2)}) async-start(s8[8388608]{0:T(1024)(128)(4,1)} %bitcast.230), calls=%async_computation.11 | async-start | bytes 8388608
  1305.4 27.4 %slice-start.7 = ((s8[8388608]{0:T(1024)(128)(4,1)}), s8[4194304]{0:T(1024)(128)(4,1)S(1)}, s32[]{:S(2)}) async-start(s8[8388608]{0:T(1024)(128)(4,1)} %bitcast.230), calls=%async_computation.12 | async-start | bytes 8388608
  1321.1 11.7 copy-start.7
Sparse Core Ops, SparseCore 0:
  1340.5 152.0 all-reduce.1
